TPU v7x, 32 devices: a whole 2x2x4 slice. The times are simulated.
32 devices in a mesh: slab: 4 (over x, core), panel: 8 (over z, y).
Axes of the slice: x: 2, y: 2, z: 4, core: 2. Of those that a mesh axis runs over, the one named last changes fastest.
Arguments:
- ranges: float32 [4, 4, 1024, 1024], P('slab', None, 'panel'), may hold values from -1.5 to 1.5
- pattern: int32 [4, 4, 16, 16], P('slab'), may hold values 0 or 1
Outputs:
- combined: float32 [4, 4, 1024, 1024], P('slab', None, 'panel')
All inputs are finite; a program needn't handle non-finite values. No bound on the sum of `pattern` on one device may be relied on, other than what follows from the above.
Results may differ from a plain program's by a relative error of at most 0.01.
Values may be sent and summed in bfloat16 or wider, within the bound.
A program may use at most 64 MiB of HBM per device.

v0:
```python
import functools
import jax
import jax.numpy as jnp
from jax import lax
from jax.experimental import pallas as pl
from jax.experimental.pallas import tpu as pltpu
from jax.sharding import PartitionSpec as P

BLK = 64
MESH = pl.DeviceIdType.MESH


def kernel(outer, inner, counts, first_ref, second_ref, left_ref, add_ref, own_ref, other_ref,
           right, swap, sums, base, front, mid, recv_sem, send_sem, swap_recv, swap_send, local_sem, last_recv, last_send):
    rows, width = left_ref.shape
    panels = outer * inner
    slab = lax.axis_index("slab")
    panel = lax.axis_index("panel")
    core = slab % 2
    side = (slab // 2) % 2
    sibling = slab + 1 - 2 * core
    partner = slab + 2 - 4 * side
    out_pos = panel // inner
    in_pos = panel % inner

    column = panel % inner
    rise = panel // inner
    spot_here = column * outer + rise + (outer - 1 - 2 * rise) * (column % 2)

    def at_ring(shift):
        where = (spot_here + shift + panels) % panels
        turn = where // outer
        step = where % outer
        return (step + (outer - 1 - 2 * step) * (turn % 2)) * inner + turn

    ahead = (slab, at_ring(1))
    behind = (slab, at_ring(-1))

    barrier = pltpu.get_barrier_semaphore()
    friends = [ahead, behind, (sibling, panel), (partner, panel)]
    for friend in friends:
        pl.semaphore_signal(barrier, inc=1, device_id=friend, device_id_type=MESH)
    pl.semaphore_wait(barrier, len(friends))

    sent = []
    piece = rows // 2
    reach = panels // 2

    def place(level, kind, owner, p, half):
        return right.at[level, kind, owner, pl.ds(pl.multiple_of(p * rows + half * piece, piece), piece), :]

    def push(level, kind, src, p, half, target, guard):
        spot = len(sent)
        sent.append(guard)
        pltpu.make_async_remote_copy(
            src_ref=src, dst_ref=place(level, kind, core, p, half), send_sem=send_sem.at[spot],
            recv_sem=recv_sem.at[level, kind, core, p, half], device_id=target, device_id_type=MESH).start()

    def arrive(level, kind, owner, p, half):
        spot = place(level, kind, owner, p, half)
        pltpu.make_async_remote_copy(
            src_ref=spot, dst_ref=spot, send_sem=send_sem.at[0], recv_sem=recv_sem.at[level, kind, owner, p, half],
            device_id=(sibling, panel), device_id_type=MESH).wait_recv()

    def share(level, kind, src, p, half, guard):
        if guard == "gives" and kind == 1:
            push(level, kind, src, p, half, (partner, panel), guard)
        push(level, kind, src, p, half, (sibling, panel), guard)

    def local_copy(level, kind, src):
        return pltpu.make_async_copy(src, right.at[level, kind, core, pl.ds(pl.multiple_of(panel * rows, rows), rows), :],
                                     local_sem.at[level, kind])

    def open_ring(level, kind, src, guard=None, ready=None):
        for half in range(2):
            if ready:
                ready(half)
            part = src.at[pl.ds(half * piece, piece), :]
            push(level, kind, part, panel, half, ahead, guard)
            push(level, kind, part, panel, half, behind, guard)
            share(level, kind, part, panel, half, guard)
        local_copy(level, kind, src).start()

    def items(distance):
        for half in range(2):
            for way in (1, -1):
                if distance < reach or (half == 0) == (way == 1):
                    passes = distance + 1 < reach or (distance + 1 == reach and (half == 0) == (way == 1))
                    yield half, way, passes

    def relay(level, kind, distance, guard=None):
        for half, way, passes in items(distance):
            p = at_ring(-way * distance)
            arrive(level, kind, core, p, half)
            src = place(level, kind, core, p, half)
            if passes:
                push(level, kind, src, p, half, ahead if way == 1 else behind, guard)
            share(level, kind, src, p, half, guard)

    def follow(level, kind, distance):
        pairs = [(half, way) for half, way, _ in items(distance)] if distance else [(0, 1), (1, 1)]
        for half, way in pairs:
            p = at_ring(-way * distance)
            arrive(level, kind, core, p, half)
            share(level, kind, place(level, kind, core, p, half), p, half, "takes")

    def settle(level, kind, distances):
        for distance in distances:
            pairs = [(half, way) for half, way, _ in items(distance)] if distance else [(0, 1), (1, 1)]
            for half, way in pairs:
                arrive(level, kind, 1 - core, at_ring(-way * distance), half)

    gives = (side + core) % 2
    slot = 1 - gives

    def product(left, factor, emit):
        @pl.loop(0, width // width)
        def _(step):
            cols = pl.ds(pl.multiple_of(step * width, width), width)
            emit(cols, jnp.dot(left[...], factor[:, cols], preferred_element_type=jnp.float32))

    def keep(ref):
        def emit(cols, value):
            ref[:, cols] = value.astype(ref.dtype)
        return emit

    def keep_sum(ref, extra):
        def emit(cols, value):
            ref[:, cols] = (extra[:, cols].astype(jnp.float32) + value).astype(ref.dtype)
        return emit

    def swap_copy(which):
        ref = swap.at[0, 0, pl.ds(which * piece, piece), :] if which < 2 else swap.at[1, 3 - which]
        return pltpu.make_async_remote_copy(
            src_ref=ref, dst_ref=ref, send_sem=swap_send.at[which],
            recv_sem=swap_recv.at[which], device_id=(partner, panel), device_id_type=MESH)

    is_tail = core == 1

    def merge(level, lead, first, second, left, add, outs, after_diag):
        def run(action):
            if level == 0:
                action(None)
            else:
                pl.when(gives == 1)(lambda: action("gives"))

        def step(distance):
            run(lambda guard: relay(level, 1, distance, guard))
            if level == 1:
                pl.when(gives == 0)(lambda: follow(level, 1, distance))

        def start_second():
            run(lambda guard: open_ring(level, 1, second, guard))
            if level == 1:
                pl.when(gives == 0)(lambda: follow(level, 1, 0))

        split = rows % 128 == 0
        if level == 0:
            open_ring(level, 0, first)
        if lead == 0:
            start_second()
        for distance in range(1, reach):
            relay(level, 0, distance)
            if distance == lead:
                start_second()
            if distance > lead:
                step(distance - lead)
        relay(level, 0, reach)
        settle(level, 0, range(reach + 1))
        local_copy(level, 0, first).wait()
        if level == 1:
            pl.when(gives == 1)(lambda: swap_copy(2).wait_recv())
        top = right.at[level, 0, 1 - level]
        bottom = right.at[level, 0, level]

        @pl.when(is_tail)
        def _():
            product(left, bottom, keep(base))

        @pl.when(core == 0)
        def _():
            base[...] = left[...]

        pending = list(range(max(reach - lead, 1), reach + 1))
        last = [pending.pop()] if split else []
        early = max(len(pending) // 4, 1)

        def some():
            for _ in range(early):
                if pending:
                    step(pending.pop(0))

        for turn in range(3):
            product(base if turn == 0 else front, top, keep(mid))
            some()
            product(mid, bottom, keep_sum(front, base))
        product(front, top, keep(mid))

        @pl.when(is_tail)
        def _():
            front[...] = (left[...].astype(jnp.float32) + mid[...].astype(jnp.float32)).astype(front.dtype)
            product(mid, bottom, keep_sum(base, base))

        @pl.when(core == 0)
        def _():
            base[...] = mid[...]

        mine = right.at[level, 1, core]
        theirs = right.at[level, 1, 1 - core]
        diag_factor, side_factor = (mine, theirs) if level == 0 else (theirs, mine)
        while pending:
            step(pending.pop(0))
        settle(level, 1, range(reach if split else reach + 1))
        run(lambda guard: local_copy(level, 1, second).wait())

        def term(left, factor, cols, p):
            span = pl.ds(pl.multiple_of(p * rows, rows), rows)
            return jnp.dot(left[:, span], factor[span, cols], preferred_element_type=jnp.float32)

        near = [0] + [way * distance for distance in range(1, reach) for way in (1, -1)]

        def partial(left, factor, out):
            @pl.loop(0, width // width)
            def _(tile):
                cols = pl.ds(pl.multiple_of(tile * width, width), width)
                out[:, cols] = sum(term(left, factor, cols, at_ring(shift)) for shift in near)

        def finish(left, factor, part, emit):
            @pl.loop(0, width // width)
            def _(tile):
                cols = pl.ds(pl.multiple_of(tile * width, width), width)
                emit(cols, part[:, cols] + term(left, factor, cols, at_ring(reach)))

        if split:
            partial(base, diag_factor, sums.at[0])
            partial(front, side_factor, sums.at[1])
            step(last[0])
            settle(level, 1, [reach])
        if level == 1:
            pl.when(gives == 1)(lambda: swap_copy(3).wait_recv())
        if split:
            finish(base, diag_factor, sums.at[0], keep_sum(outs[0], add))
            after_diag()
            finish(front, side_factor, sums.at[1], keep(outs[1]))
        else:
            product(base, diag_factor, keep_sum(outs[0], add))
            after_diag()
            product(front, side_factor, keep(outs[1]))

    def give():
        for half in range(2):
            swap_copy(half).start()
        open_ring(1, 0, swap.at[0, 0], "gives")

    def take():
        swap_copy(2).start()
        open_ring(1, 0, swap.at[0, 0], "takes", lambda half: swap_copy(half).wait_recv())
        swap_copy(3).start()

    merge(0, 1, first_ref, second_ref, left_ref, add_ref,
          (swap.at[slot, 0], swap.at[slot, 1]), lambda: pl.when(gives == 1)(give))
    pl.when(gives == 0)(take)

    def last_copy(kind):
        return pltpu.make_async_remote_copy(
            src_ref=own_ref.at[kind], dst_ref=other_ref.at[kind], send_sem=last_send.at[kind],
            recv_sem=last_recv.at[kind], device_id=(sibling, panel), device_id_type=MESH)

    merge(1, 0, swap.at[0, 0], swap.at[0, 1], swap.at[1, 1], swap.at[1, 0],
          (own_ref.at[0], own_ref.at[1]), lambda: last_copy(0).start())
    last_copy(1).start()

    @pl.when(gives == 1)
    def _():
        for which in (0, 1):
            swap_copy(which).wait_send()

    @pl.when(gives == 0)
    def _():
        for which in (2, 3):
            swap_copy(which).wait_send()

    def drain(guard):
        own = right.at[0, 0, 0, pl.ds(0, piece), :]
        for spot, kept in enumerate(sent):
            if kept == guard:
                pltpu.make_async_remote_copy(
                    src_ref=own, dst_ref=own, send_sem=send_sem.at[spot], recv_sem=recv_sem.at[0, 0, 0, 0, 0],
                    device_id=(sibling, panel), device_id_type=MESH).wait_send()

    drain(None)
    pl.when(gives == 1)(lambda: drain("gives"))
    pl.when(gives == 0)(lambda: drain("takes"))
    for kind in range(2):
        last_copy(kind).wait()
    assert len(sent) <= counts, len(sent)


def body(panels, ranges, pattern):
    blocks = ranges[0]
    rows, width = blocks.shape[1:]
    count = pattern.shape[2]
    core = lax.axis_index("slab") % 2
    row_start = lax.axis_index("panel") * rows
    row_ids = row_start + jnp.arange(rows, dtype=jnp.int32)
    col_ids = jnp.arange(width, dtype=jnp.int32)
    block_ids = jnp.arange(count, dtype=jnp.int32)
    row_pick = (row_ids[:, None] // BLK == block_ids[None, :]).astype(jnp.float32)
    col_pick = (block_ids[:, None] == col_ids[None, :] // BLK).astype(jnp.float32)
    mask = jnp.einsum("mi,gij,jc->gmc", row_pick, pattern[0].astype(jnp.float32), col_pick)
    masked = blocks * mask
    half = masked.astype(jnp.bfloat16)
    head = core == 0
    first = jnp.where(head, half[3], half[0])
    second = jnp.where(head, half[2], half[1])
    left = jnp.where(head, half[1], half[2])
    add = jnp.where(head, masked[0], masked[3])

    outer = min(4, panels)
    inner = panels // outer
    counts = 24 * panels
    vmem = pl.BlockSpec(memory_space=pltpu.VMEM)
    own, other = pl.pallas_call(
        functools.partial(kernel, outer, inner, counts),
        out_shape=[jax.ShapeDtypeStruct((2, rows, width), jnp.float32)] * 2,
        in_specs=[vmem] * 4,
        out_specs=[vmem] * 2,
        scratch_shapes=[
            pltpu.VMEM((2, 2, 2, width, width), jnp.bfloat16),
            pltpu.VMEM((2, 2, rows, width), jnp.bfloat16),
            pltpu.VMEM((2, rows, width), jnp.float32),
            pltpu.VMEM((rows, width), jnp.bfloat16),
            pltpu.VMEM((rows, width), jnp.bfloat16),
            pltpu.VMEM((rows, width), jnp.bfloat16),
            pltpu.SemaphoreType.DMA((2, 2, 2, panels, 2)),
            pltpu.SemaphoreType.DMA((counts,)),
            pltpu.SemaphoreType.DMA((4,)),
            pltpu.SemaphoreType.DMA((4,)),
            pltpu.SemaphoreType.DMA((2, 2)),
            pltpu.SemaphoreType.DMA((2,)),
            pltpu.SemaphoreType.DMA((2,)),
        ],
        compiler_params=pltpu.CompilerParams(
            collective_id=0, has_side_effects=True, vmem_limit_bytes=48 << 20),
        name="merge_levels",
    )(first, second, left, add)
    return jnp.stack([
        jnp.where(head, own[0], other[0]),
        jnp.where(head, own[1], other[1]),
        jnp.where(head, other[1], own[1]),
        jnp.where(head, other[0], own[0]),
    ])[None]


def solution(mesh):
    return jax.shard_map(
        functools.partial(body, mesh.shape["panel"]),
        mesh=mesh,
        in_specs=(P("slab", None, "panel", None), P("slab", None, None, None)),
        out_specs=P("slab", None, "panel", None),
        check_vma=False,
    )
```

profile of v0, /device:TPU:0, one launch (start us, length us, event | category | flops | bytes accessed | tf_op | source)
XLA Modules:
  0.0 100.7 jit_solution(11441111671285838568)
XLA Ops:
  0.0 2.3 %fusion.17 = (bf16[4,128,1024]{2,1,0:T(8,128)(2,1)S(1)}, f32[4,128,1024]{2,1,0:T(8,128)S(1)}) fusion(s32[1024]{0:T(1024)S(1)} %add_select_fusion, s32[1,4,16,16]{3,2,1,0:T(8,128)} %param.3, s32[128]{0:T(128)S(1)} %and_select_fusion, f32[1,4,128,1024]{3,2,1,0:T(8,128)} %param.2), kind=kOutput, calls=%fused_computation.32 | convolution fusion | flops 18107392 | bytes 5251584 | tf_op jit(solution)/shard_map/mi,gij,jc->gmc/dot_general | solution.py:310
  2.3 0.1 select_bitcast_fusion
  2.4 0.1 fusion.add_ref
  2.5 96.6 %merge_levels.1 = (f32[2,128,1024]{2,1,0:T(8,128)S(1)}, f32[2,128,1024]{2,1,0:T(8,128)S(1)}) custom-call(bf16[128,1024]{1,0:T(8,128)(2,1)S(1)} %get-tuple-element.15.first_ref, bf16[128,1024]{1,0:T(8,128)(2,1)S(1)} %get-tuple-element.14.second_ref, bf16[128,1024]{1,0:T(8,128)(2,1)S(1)} %get-tuple-element.13.left_ref, f32[128,1024]{1,0:T(8,128)S(1)} %fusion.add_ref), custom_call_target="tpu_custom_call" | custom-call | tf_op jit(solution)/shard_map/merge_levels/pallas_call | solution.py:323
  99.0 0.2 slice_select_fusion.4
  99.2 1.5 %maximum_bitcast_fusion = f32[1,4,128,1024]{3,2,1,0:T(8,128)} fusion(f32[1,128,1024]{2,1,0:T(8,128)S(1)} %get-tuple-element.10, f32[1,128,1024]{2,1,0:T(8,128)S(1)} %get-tuple-element.11, f32[1,128,1024]{2,1,0:T(8,128)S(1)} %get-tuple-element.12, f32[1,128,1024]{2,1,0:T(8,128)S(1)} %get-tuple-element.9), kind=kLoop, calls=%fused_computation | loop fusion | flops 1572864 | bytes 4194304 | tf_op jit(solution)/shard_map/broadcast_in_dim | solution.py:347
  (2 shorter events, 0.0 us)
where the time goes:
time: 101 us
  Pallas kernels  96.6 us (96%)
  matrix products  2.3 us (2%)
  other arithmetic  1.76 us (2%)
    pallas_call x1, Pallas kernels, body(): pl.pallas_call(functools.partial(kernel, outer, inner, counts), out_shape...  96.6 us
    dot_general x1, matrix products, body(): jnp.einsum('mi,gij,jc->gmc', row_pick, pattern[0].astype(jnp.float32), co...  2.3 us

commit v1 on v0

v1 whole, which is shorter than its diff:
```python
import functools
import jax
import jax.numpy as jnp
from jax import lax
from jax.experimental import pallas as pl
from jax.experimental.pallas import tpu as pltpu
from jax.sharding import PartitionSpec as P

BLK = 64
MESH = pl.DeviceIdType.MESH


def merged(*streams):
    events = []
    for order, (items, start, end) in enumerate(streams):
        for i, item in enumerate(items):
            events.append((start + (end - start) * (i + 0.5) / len(items), order, i, item))
    return [event[-1] for event in sorted(events, key=lambda event: event[:3])]


def kernel(outer, inner, counts, first_ref, second_ref, left_ref, add_ref, out_ref,
           right, swap, hold, base, front, mid, recv_sem, send_sem, swap_sem, local_sem, last_recv, last_send):
    rows, width = left_ref.shape
    panels = outer * inner
    reach = panels // 2
    piece = rows // 2
    wing = width // 2
    slab = lax.axis_index("slab")
    panel = lax.axis_index("panel")
    core = slab % 2
    side = (slab // 2) % 2
    chip = slab - core
    far_chip = chip + 2 - 4 * side
    sibling = (chip + 1 - core, panel)
    partner = (far_chip + core, panel)
    gives = (side + core) % 2
    turn_way = 1 - 2 * core
    is_tail = core == 1
    is_giver = gives == 1
    is_taker = gives == 0

    column = panel % inner
    rise = panel // inner
    spot_here = column * outer + rise + (outer - 1 - 2 * rise) * (column % 2)

    def at_ring(shift):
        where = (spot_here + shift + panels) % panels
        turn = where // outer
        step = where % outer
        return (step + (outer - 1 - 2 * step) * (turn % 2)) * inner + turn

    beside = {1: at_ring(1), -1: at_ring(-1)}

    barrier = pltpu.get_barrier_semaphore()
    friends = [(chip + half, beside[way]) for way in (1, -1) for half in range(2)]
    friends += [(far_chip + half, panel) for half in range(2)] + [sibling]
    for friend in friends:
        pl.semaphore_signal(barrier, inc=1, device_id=friend, device_id_type=MESH)
    pl.semaphore_wait(barrier, len(friends))

    sent = []
    LATE, REST = 3, 7
    wings = {LATE: 0, REST: wing}

    def block(m, row, count):
        span = pl.ds(pl.multiple_of(row, count), count)
        if isinstance(m, int) and m in wings:
            return right.at[LATE, span, pl.ds(wings[m], wing)]
        return right.at[m, span, :]

    def place(m, p, half):
        return block(m, p * rows + half * piece, piece)

    def own_rows(m):
        return block(m, panel * rows, rows)

    def push(m, src, p, half, target, guard=None):
        spot = len(sent)
        sent.append((guard, m))
        pltpu.make_async_remote_copy(
            src_ref=src, dst_ref=place(m, p, half), send_sem=send_sem.at[spot],
            recv_sem=recv_sem.at[m, p, half], device_id=target, device_id_type=MESH).start()

    def arrive(m, p, half):
        spot = place(m, p, half)
        pltpu.make_async_remote_copy(
            src_ref=spot, dst_ref=spot, send_sem=send_sem.at[0], recv_sem=recv_sem.at[m, p, half],
            device_id=sibling, device_id_type=MESH).wait_recv()

    def local_copy(m, src):
        return pltpu.make_async_copy(src, own_rows(m), local_sem.at[m])

    def open_ring(m, src, guard=None, across=False):
        parts = [src.at[pl.ds(half * piece, piece), :] for half in range(2)]
        for half in range(2):
            for way in (1, -1):
                push(m, parts[half], panel, half, (chip + half, beside[way]), guard)
            if across:
                push(m, parts[half], panel, half, (far_chip + half, panel), guard)
        for half in range(2):
            push(m, parts[half], panel, half, sibling, guard)

    def spread(distance):
        return [turn_way, -turn_way] if distance < reach else [turn_way]

    def relay(m, distance, across=False):
        for i, way in enumerate(spread(distance)):
            p = at_ring(-way * distance)
            arrive(m, p, core)
            src = place(m, p, core)
            if distance + 1 < reach or (distance + 1 == reach and i == 0):
                push(m, src, p, core, (slab, at_ring(way)))
            if across:
                push(m, src, p, core, partner)
            push(m, src, p, core, sibling)

    def relay_far(m, distance):
        for way in spread(distance) if distance else [1]:
            p = at_ring(-way * distance)
            arrive(m, p, core)
            push(m, place(m, p, core), p, core, sibling)

    def settle(m, far=False):
        if far:
            arrive(m, panel, 1 - core)
        for distance in range(1, reach + 1):
            for way in (1, -1) if distance < reach else (1,):
                arrive(m, at_ring(-way * distance), 1 - core)

    def settle_own(m, absent):
        @pl.when(absent)
        def _():
            for half in range(2):
                arrive(m, panel, half)

    def product(left, factor, emit, cols=None):
        cols = slice(None) if cols is None else cols
        emit(cols, jnp.dot(left[...], factor[:, cols], preferred_element_type=jnp.float32))

    def keep(ref):
        def emit(cols, value):
            ref[:, cols] = value.astype(ref.dtype)
        return emit

    def keep_sum(ref, extra):
        def emit(cols, value):
            ref[:, cols] = (extra[:, cols].astype(jnp.float32) + value).astype(ref.dtype)
        return emit

    def swap_copy():
        return pltpu.make_async_remote_copy(
            src_ref=swap, dst_ref=swap, send_sem=swap_sem.at[0],
            recv_sem=swap_sem.at[1], device_id=partner, device_id_type=MESH)

    def chain(left, top, bottom, work, kept):
        count = len(work)

        def some(turn):
            while work and len(work) > count - (turn + 1) * count // 4:
                work.pop(0)()

        @pl.when(is_tail)
        def _():
            product(left, bottom, keep(base))

        @pl.when(core == 0)
        def _():
            base[...] = left[...]

        for turn in range(3):
            product(base if turn == 0 else front, top, keep(mid))
            some(turn)
            product(mid, bottom, keep_sum(front, base))
        product(front, top, keep(mid))
        some(3)

        @pl.when(is_tail)
        def _():
            front[...] = (left[...].astype(jnp.float32) + mid[...].astype(jnp.float32)).astype(front.dtype)
            product(mid, bottom, keep_sum(kept, base))

        @pl.when(core == 0)
        def _():
            kept[...] = mid[...]

    def later(action, *args):
        return lambda: action(*args)

    def relays(m, start, end):
        return [later(relay, m, distance) for distance in range(start, end)]

    def run(actions):
        for action in actions:
            action()

    def open_early():
        @pl.when(is_giver)
        def _():
            open_ring(2, second_ref, "gives")
            local_copy(2, second_ref).start()

    def open_late(m):
        @pl.when(is_taker)
        def _():
            part = second_ref.at[:, pl.ds(wings[m], wing)]
            open_ring(m, part, "takes")
            local_copy(m, part).start()

    quarter = max(reach // 4, 1)
    open_ring(core, first_ref)
    local_copy(core, first_ref).start()
    run(merged(
        ([later(relay, m, distance) for distance in range(1, reach + 1) for m in range(2)], 0, 1),
        ([open_early], 0.4, 0.5), (relays(2, 1, quarter + 1), 0.7, 0.8), ([later(open_late, LATE)], 0.75, 0.8)))
    for m in range(2):
        settle(m)
    local_copy(core, first_ref).wait()
    for half in range(2):
        arrive(1 - core, panel, half)
    chain(left_ref, right.at[1], right.at[0], merged(
        (relays(2, quarter + 1, 3 * quarter + 1), 0, 1), (relays(LATE, 1, quarter + 1), 0.3, 0.7)), hold)
    mine, far, extra = 4 + side, 5 - side, 6

    @pl.when(is_giver)
    def _():
        own_rows(extra)[...] = front[...]
        open_ring(extra, own_rows(extra), "gives")

    run(merged(
        (relays(2, 3 * quarter + 1, reach + 1), 0, 1), (relays(LATE, quarter + 1, 2 * quarter + 1), 0, 0.5)))
    settle(2)
    settle_own(2, is_taker)

    @pl.when(is_giver)
    def _():
        local_copy(2, second_ref).wait()
        product(hold, right.at[2], keep_sum(own_rows(mine), add_ref))
        open_ring(mine, own_rows(mine), "gives", True)

    @pl.when(is_taker)
    def _():
        product(front, right.at[2], keep(swap))
        swap_copy().start()

    kind = [later(relay, mine, 1, True), later(relay_far, far, 0)]
    for distance in range(2, reach + 1):
        kind += [later(relay, mine, distance, True), later(relay_far, far, distance - 1)]
    kind += [later(relay_far, far, reach)]
    run(merged(
        (kind, 0, 1), (relays(extra, 1, 3 * quarter + 1), 0, 0.8), (relays(LATE, 2 * quarter + 1, reach + 1), 0, 0.5),
        ([later(open_late, REST)] + relays(REST, 1, 2 * quarter + 1), 0.2, 1)))
    settle(mine)
    settle(far, True)
    settle_own(mine, is_taker)

    @pl.when(is_giver)
    def _():
        swap_copy().wait_recv()

    chain(swap, right.at[5], right.at[4], merged((relays(extra, 3 * quarter + 1, reach + 1), 0, 1), (relays(REST, 2 * quarter + 1, 3 * quarter + 1), 0, 1)), base)
    run([])
    settle(extra)
    settle_own(extra, is_taker)

    @pl.when(is_giver)
    def _():
        product(front, right.at[extra], keep(mid))

    @pl.when(is_taker)
    def _():
        product(base, right.at[extra], keep_sum(mid, hold))

    here = 2 * core + side
    across = 2 * core + 1 - side

    def last_copy(m, kind):
        cols = pl.ds(wings[m], wing)
        spot = 3 * (m == REST) + kind
        ref = out_ref.at[across if kind == 2 else here, :, cols]
        return pltpu.make_async_remote_copy(
            src_ref=ref, dst_ref=ref, send_sem=last_send.at[spot], recv_sem=last_recv.at[spot],
            device_id=partner if kind == 0 else sibling, device_id_type=MESH)

    for m in (LATE, REST):
        if m == REST:
            run(relays(REST, 3 * quarter + 1, reach + 1))
        settle(m)
        settle_own(m, is_giver)
        cols = slice(wings[m], wings[m] + wing)

        @pl.when(is_giver)
        def _():
            product(mid, right.at[LATE], keep(out_ref.at[here]), cols)

        @pl.when(is_taker)
        def _():
            local_copy(m, second_ref.at[:, pl.ds(wings[m], wing)]).wait()
            product(mid, right.at[LATE], keep_sum(out_ref.at[here], add_ref), cols)

        last_copy(m, 0).start()
        last_copy(m, 1).start()
    for m in (LATE, REST):
        last_copy(m, 0).wait_recv()
        last_copy(m, 2).start()

    @pl.when(is_taker)
    def _():
        swap_copy().wait_send()

    def drain(guard):
        for spot, (kept, m) in enumerate(sent):
            if kept == guard:
                own = place(m if isinstance(m, int) else 0, 0, 0)
                pltpu.make_async_remote_copy(
                    src_ref=own, dst_ref=own, send_sem=send_sem.at[spot], recv_sem=recv_sem.at[0, 0, 0],
                    device_id=sibling, device_id_type=MESH).wait_send()

    drain(None)
    pl.when(is_giver)(lambda: drain("gives"))
    pl.when(is_taker)(lambda: drain("takes"))
    for m in (LATE, REST):
        last_copy(m, 0).wait_send()
        last_copy(m, 1).wait()
        last_copy(m, 2).wait()
    assert len(sent) <= counts, len(sent)


def body(panels, ranges, pattern):
    blocks = ranges[0]
    rows, width = blocks.shape[1:]
    count = pattern.shape[2]
    core = lax.axis_index("slab") % 2
    row_start = lax.axis_index("panel") * rows
    row_ids = row_start + jnp.arange(rows, dtype=jnp.int32)
    col_ids = jnp.arange(width, dtype=jnp.int32)
    block_ids = jnp.arange(count, dtype=jnp.int32)
    row_pick = (row_ids[:, None] // BLK == block_ids[None, :]).astype(jnp.float32)
    col_pick = (block_ids[:, None] == col_ids[None, :] // BLK).astype(jnp.float32)
    mask = jnp.einsum("mi,gij,jc->gmc", row_pick, pattern[0].astype(jnp.float32), col_pick)
    masked = blocks * mask
    half = masked.astype(jnp.bfloat16)
    head = core == 0
    first = jnp.where(head, half[3], half[0])
    second = jnp.where(head, half[2], half[1])
    left = jnp.where(head, half[1], half[2])
    add = jnp.where(head, masked[0], masked[3])

    outer = min(4, panels)
    inner = panels // outer
    counts = 24 * panels
    vmem = pl.BlockSpec(memory_space=pltpu.VMEM)
    out = pl.pallas_call(
        functools.partial(kernel, outer, inner, counts),
        out_shape=jax.ShapeDtypeStruct((4, rows, width), jnp.bfloat16),
        in_specs=[vmem] * 4,
        out_specs=vmem,
        scratch_shapes=[
            pltpu.VMEM((7, width, width), jnp.bfloat16),
            *[pltpu.VMEM((rows, width), jnp.bfloat16)] * 5,
            pltpu.SemaphoreType.DMA((8, panels, 2)),
            pltpu.SemaphoreType.DMA((counts,)),
            pltpu.SemaphoreType.DMA((2,)),
            pltpu.SemaphoreType.DMA((8,)),
            pltpu.SemaphoreType.DMA((6,)),
            pltpu.SemaphoreType.DMA((6,)),
        ],
        compiler_params=pltpu.CompilerParams(
            collective_id=0, has_side_effects=True, vmem_limit_bytes=48 << 20),
        name="merge_levels",
    )(first, second, left, add)
    return out.astype(jnp.float32)[None]


def solution(mesh):
    return jax.shard_map(
        functools.partial(body, mesh.shape["panel"]),
        mesh=mesh,
        in_specs=(P("slab", None, "panel", None), P("slab", None, None, None)),
        out_specs=P("slab", None, "panel", None),
        check_vma=False,
    )
```

time: 101 us -> 91.4 us (0.905)
  Pallas kernels: 96.6 us -> 87.2 us
    pallas_call x1, Pallas kernels: 96.6 us -> 87.2 us  [body(): pl.pallas_call(functools.partial(kernel, outer, inner, counts), out_shape...]
where the time goes in v1:
time: 91.4 us; the launch traced here: 91.2 us
  Pallas kernels  87.2 us (95%)
  matrix products  2.3 us (3%)
  other arithmetic  1.7 us (2%)
    pallas_call x1, Pallas kernels, body(): pl.pallas_call(functools.partial(kernel, outer, inner, counts), out_shape...  87.2 us
    dot_general x1, matrix products, body(): jnp.einsum('mi,gij,jc->gmc', row_pick, pattern[0].astype(jnp.float32), co...  2.3 us

profile of v1, /device:TPU:0, one launch (start us, length us, event | category | flops | bytes accessed | tf_op | source)
XLA Modules:
  0.0 91.2 jit_solution(18172378395370431130)
XLA Ops:
  0.0 2.3 %fusion.17 = (bf16[4,128,1024]{2,1,0:T(8,128)(2,1)S(1)}, f32[4,128,1024]{2,1,0:T(8,128)S(1)}) fusion(s32[1024]{0:T(1024)S(1)} %add_select_fusion, s32[1,4,16,16]{3,2,1,0:T(8,128)} %param.3, s32[128]{0:T(128)S(1)} %and_select_fusion, f32[1,4,128,1024]{3,2,1,0:T(8,128)} %param.2), kind=kOutput, calls=%fused_computation.28 | convolution fusion | flops 18107392 | bytes 5251584 | tf_op jit(solution)/shard_map/mi,gij,jc->gmc/dot_general | solution.py:339
  2.3 0.1 select_bitcast_fusion
  2.4 0.1 fusion.add_ref
  2.5 87.2 %merge_levels.1 = bf16[4,128,1024]{2,1,0:T(8,128)(2,1)S(1)} custom-call(bf16[128,1024]{1,0:T(8,128)(2,1)S(1)} %get-tuple-element.7.first_ref, bf16[128,1024]{1,0:T(8,128)(2,1)S(1)} %get-tuple-element.6.second_ref, bf16[128,1024]{1,0:T(8,128)(2,1)S(1)} %get-tuple-element.5.left_ref, f32[128,1024]{1,0:T(8,128)S(1)} %fusion.add_ref), custom_call_target="tpu_custom_call" | custom-call | tf_op jit(solution)/shard_map/merge_levels/pallas_call | solution.py:352
  89.7 1.6 %bitcast_convert_fusion = f32[1,4,128,1024]{3,2,1,0:T(8,128)} fusion(bf16[4,128,1024]{2,1,0:T(8,128)(2,1)S(1)} %merge_levels.1), kind=kLoop, calls=%fused_computation.2 | loop fusion | flops 524288 | bytes 3145728 | tf_op jit(solution)/shard_map/broadcast_in_dim | solution.py:371
  (2 shorter events, 0.0 us)

commit v2 on v1

--- a/solution.py
+++ b/solution.py
@@ -110,15 +110,25 @@
             src = place(m, p, core)
             if distance + 1 < reach or (distance + 1 == reach and i == 0):
                 push(m, src, p, core, (slab, at_ring(way)))
-            if across:
+            if across and not by_ring(distance):
                 push(m, src, p, core, partner)
             push(m, src, p, core, sibling)
 
+    def by_ring(distance):
+        return distance == reach
+
     def relay_far(m, distance):
-        for way in spread(distance) if distance else [1]:
+        for i, way in enumerate(spread(distance) if distance else [1]):
             p = at_ring(-way * distance)
             arrive(m, p, core)
-            push(m, place(m, p, core), p, core, sibling)
+            src = place(m, p, core)
+            if by_ring(distance + 1):
+                if distance == 0:
+                    push(m, src, p, core, (slab, beside[1]))
+                    push(m, src, p, core, (slab, beside[-1]))
+                elif distance + 1 < reach or (distance + 1 == reach and i == 0):
+                    push(m, src, p, core, (slab, at_ring(way)))
+            push(m, src, p, core, sibling)
 
     def settle(m, far=False):
         if far:

time: 91.4 us -> 90.1 us (0.986)
  Pallas kernels: 87.2 us -> 85.9 us
    pallas_call x1, Pallas kernels: 87.2 us -> 85.9 us  [body(): pl.pallas_call(functools.partial(kernel, outer, inner, counts), out_shape...]
where the time goes in v2:
time: 90.1 us; the launch traced here: 90 us
  Pallas kernels  85.9 us (95%)
  matrix products  2.3 us (3%)
  other arithmetic  1.7 us (2%)
    pallas_call x1, Pallas kernels, body(): pl.pallas_call(functools.partial(kernel, outer, inner, counts), out_shape...  85.9 us
    dot_general x1, matrix products, body(): jnp.einsum('mi,gij,jc->gmc', row_pick, pattern[0].astype(jnp.float32), co...  2.3 us

profile of v2, /device:TPU:0, one launch (start us, length us, event | category | flops | bytes accessed | tf_op | source)
XLA Modules:
  0.0 90.0 jit_solution(5709734770668116052)
XLA Ops:
  0.0 2.3 %fusion.17 = (bf16[4,128,1024]{2,1,0:T(8,128)(2,1)S(1)}, f32[4,128,1024]{2,1,0:T(8,128)S(1)}) fusion(s32[1024]{0:T(1024)S(1)} %add_select_fusion, s32[1,4,16,16]{3,2,1,0:T(8,128)} %param.3, s32[128]{0:T(128)S(1)} %and_select_fusion, f32[1,4,128,1024]{3,2,1,0:T(8,128)} %param.2), kind=kOutput, calls=%fused_computation.28 | convolution fusion | flops 18107392 | bytes 5251584 | tf_op jit(solution)/shard_map/mi,gij,jc->gmc/dot_general | solution.py:349
  2.3 0.1 select_bitcast_fusion
  2.4 0.1 fusion.add_ref
  2.5 85.9 %merge_levels.1 = bf16[4,128,1024]{2,1,0:T(8,128)(2,1)S(1)} custom-call(bf16[128,1024]{1,0:T(8,128)(2,1)S(1)} %get-tuple-element.7.first_ref, bf16[128,1024]{1,0:T(8,128)(2,1)S(1)} %get-tuple-element.6.second_ref, bf16[128,1024]{1,0:T(8,128)(2,1)S(1)} %get-tuple-element.5.left_ref, f32[128,1024]{1,0:T(8,128)S(1)} %fusion.add_ref), custom_call_target="tpu_custom_call" | custom-call | tf_op jit(solution)/shard_map/merge_levels/pallas_call | solution.py:362
  88.4 1.6 %bitcast_convert_fusion = f32[1,4,128,1024]{3,2,1,0:T(8,128)} fusion(bf16[4,128,1024]{2,1,0:T(8,128)(2,1)S(1)} %merge_levels.1), kind=kLoop, calls=%fused_computation.2 | loop fusion | flops 524288 | bytes 3145728 | tf_op jit(solution)/shard_map/broadcast_in_dim | solution.py:381
  (2 shorter events, 0.0 us)
